TPU v7x, 32 devices: a whole 2x2x4 slice. The times are simulated.
32 devices in a mesh: wave: 4 (over z), tile: 8 (over y, x, core).
Axes of the slice: x: 2, y: 2, z: 4, core: 2. Of those that a mesh axis runs over, the one named last changes fastest.
Arguments:
- initial_fields: bfloat16 [16, 8, 256, 1024], P('wave', None, 'tile'), may hold values from -6 to 6
- conductivity: float32 [256, 1024], P('tile'), may hold values from 0.1 to 10
- wavenumbers: float32 [16], replicated, may hold values from 0.05 to 1.5
- quad_weights: float32 [16], replicated, may hold values from 0.05 to 0.3
- sweep_counts: int32 [16], replicated, may hold values from 1 to 8, as said below
- electrode_cells: int32 [64], replicated, may hold values from 0 to 255
- source_pairs: int32 [8, 2], replicated, may hold values from 0 to 63, as said below
Outputs:
- potential: float32 [8, 256, 1024], P('wave', 'tile')
Inputs may be any that keep to these rules, and one draw needn't show every extreme that they name: `sweep_counts`: each wavenumber gets at least one sweep and at most 8. `source_pairs`: the two electrodes of a source column are different electrodes.
All inputs are finite; a program needn't handle non-finite values.
Results may differ from a plain program's by a relative error of at most 0.0003.
Values may be sent and summed in bfloat16 or wider, within the bound.
No kernel may reach another device: no remote copies, remote signals or barrier semaphores. Data moves between devices by JAX's collectives and lax.ppermute only.
A program may use at most 64 MiB of HBM per device.

v0:
```python
import jax
import jax.numpy as jnp
from jax import lax
from jax.sharding import PartitionSpec as P

ITERS = 8


LOWER = 0.1
UPPER = 2.0
THETA = (UPPER + LOWER) / 2.0
DELTA = (UPPER - LOWER) / 2.0
SIGMA_ONE = THETA / DELTA
CURRENT = 2.0


def with_halo(block, sides, width):
    for axis, dim in sides:
        count = lax.axis_size(axis)
        forward = [(i, i + 1) for i in range(count - 1)]
        backward = [(target, source) for source, target in forward]
        low = lax.ppermute(
            lax.slice_in_dim(block, block.shape[dim] - width, None, axis=dim), axis, forward
        )
        high = lax.ppermute(lax.slice_in_dim(block, 0, width, axis=dim), axis, backward)
        block = jnp.concatenate([low, block, high], axis=dim)
    return block


def neighbours(padded_rows, facets):
    face_north, face_south, face_west, face_east = facets
    centre = padded_rows[:, 1:-1]
    columns = jnp.pad(centre, ((0, 0), (0, 0), (1, 1)))
    total = face_north * padded_rows[:, :-2] + face_south * padded_rows[:, 2:]
    return total + face_west * columns[:, :, :-2] + face_east * columns[:, :, 2:]


def chebyshev_step(step, field, direction, rho_prev, residual, diag_k, active):
    scaled = residual / diag_k
    rho_next = 1.0 / (2.0 * SIGMA_ONE - rho_prev)
    first = step == 0
    keep = jnp.where(first, 0.0, rho_next * rho_prev)
    gain = jnp.where(first, 1.0 / THETA, 2.0 * rho_next / DELTA)
    moved = keep * direction + gain * scaled
    new_rho = jnp.where(first, 1.0 / SIGMA_ONE, rho_next)
    return (
        jnp.where(active, field + moved, field),
        jnp.where(active, moved, direction),
        jnp.where(active, new_rho, rho_prev),
    )


def local(
    initial_fields,
    conductivity,
    wavenumbers,
    quad_weights,
    sweep_counts,
    electrode_cells,
    source_pairs,
):
    row_count, col_count = conductivity.shape
    tile_pos = lax.axis_index("tile")
    wave_pos = lax.axis_index("wave")
    padded_cond = with_halo(conductivity, (("tile", 0),), 1)
    padded_full = jnp.pad(padded_cond, ((0, 0), (1, 1)))
    face_north = 0.5 * (conductivity + padded_full[:-2, 1:-1])
    face_south = 0.5 * (conductivity + padded_full[2:, 1:-1])
    face_west = 0.5 * (conductivity + padded_full[1:-1, :-2])
    face_east = 0.5 * (conductivity + padded_full[1:-1, 2:])
    facets = (face_north, face_south, face_west, face_east)
    diagonal = face_north + face_south + face_west + face_east
    per_group = initial_fields.shape[0]
    wave_values = lax.dynamic_slice_in_dim(wavenumbers, wave_pos * per_group, per_group)
    weights = lax.dynamic_slice_in_dim(quad_weights, wave_pos * per_group, per_group)
    counts = lax.dynamic_slice_in_dim(sweep_counts, wave_pos * per_group, per_group)
    wave_count = initial_fields.shape[0]
    source_count = initial_fields.shape[1]
    matches = (
        source_pairs[:, :, None]
        == jnp.arange(electrode_cells.shape[0], dtype=jnp.int32)[None, None, :]
    )
    electrode_rows = jnp.sum(jnp.where(matches, electrode_cells[None, None, :], 0), axis=2)
    column_one = (jnp.arange(col_count, dtype=jnp.int32) == 0).astype(jnp.float32)
    row_ids = tile_pos * row_count + jnp.arange(row_count, dtype=jnp.int32)
    positive = (row_ids[None, :] == electrode_rows[:, 0:1]).astype(jnp.float32)
    negative = (row_ids[None, :] == electrode_rows[:, 1:2]).astype(jnp.float32)
    sources = CURRENT * (positive - negative)[:, :, None] * column_one[None, None, :]
    stacked = initial_fields.reshape(wave_count * source_count, row_count, col_count).astype(
        jnp.float32
    )
    squares = jnp.repeat(wave_values * wave_values, source_count)[:, None, None]
    per_row = jnp.repeat(counts, source_count)[:, None, None]
    active = lambda step: step < per_row
    limit = jnp.max(counts)
    source_terms = jnp.tile(sources, (wave_count, 1, 1))
    diag_k = diagonal[None] + squares * conductivity[None]

    def sweep(step, carry):
        field_now, dir_now, rho_now = carry
        padded = with_halo(field_now, (("tile", 1),), 1)
        residual = source_terms - (diag_k * field_now - neighbours(padded, facets))
        live = jnp.logical_and(active(step), step < limit)
        return chebyshev_step(step, field_now, dir_now, rho_now, residual, diag_k, live)

    rho_start = jnp.full((stacked.shape[0], 1, 1), 1.0 / SIGMA_ONE, jnp.float32)
    solved = lax.fori_loop(0, ITERS, sweep, (stacked, jnp.zeros_like(stacked), rho_start))[0]
    summed = jnp.sum(
        solved.reshape(wave_count, source_count, row_count, col_count)
        * weights[:, None, None, None],
        axis=0,
    )
    return lax.psum_scatter(summed, "wave", scatter_dimension=0, tiled=True)


def solution(mesh):
    placed = (P("wave", None, "tile", None), P("tile", None), P(), P(), P(), P(), P())
    return jax.shard_map(
        local, mesh=mesh, in_specs=placed, out_specs=P("wave", "tile", None), check_vma=False
    )
```

profile of v0, /device:TPU:0, one launch (start us, length us, event | category | flops | bytes accessed | tf_op | source)
XLA Modules:
  0.0 298.6 jit_solution(2324182616157636176)
XLA Ops:
  7.4 2.4 collective-permute-start.2
  12.0 4.0 %bitcast_convert_fusion = f32[32,32,1024]{2,1,0:T(8,128)} fusion(bf16[4,8,32,1024]{3,2,1,0:T(8,128)(2,1)} %param.9), kind=kLoop, calls=%fused_computation.33 | loop fusion | flops 1048576 | bytes 6291456 | tf_op jit(solution)/shard_map/convert_element_type | solution.py:89
  17.7 230.4 %while.20 = (s32[]{:T(128)}, f32[32,32,1024]{2,1,0:T(8,128)}, f32[32,32,1024]{2,1,0:T(8,128)}, f32[32,1,1]{0,2,1:T(1,128)S(1)}, s32[]{:T(128)}, /*index=5*/f32[3...) while((s32[]{:T(128)}, f32[32,32,1024]{2,1,0:T(8,128)}, ...), condition=%wide.region_3.4_spmd.clone, body=%wide.region_2.3_spmd.clone.sunk | while | flops 23069124 | bytes 66587184 | solution.py:107
  20.7 5.8 %collective-permute-start.1 = (f32[32,1,1024]{2,1,0:T(1,128)S(1)}, f32[32,1,1024]{2,1,0:T(1,128)S(1)}, u32[]{:S(2)}, u32[]{:S(2)}) collective-permute-start(f32[32,1,1024]{2,1,0:T(1,128)S(1)} %get-tuple-element.490), channel_id=1, source_target_pairs={{0,1},{1,2},{2,3},{3,4},{4,5},{5,6},{6,7},{8,9},{9,10},{10,11},{11... | collective-permute-start | bytes 393224 | tf_op jit(solution)/shard_map/while/body/eval_jaxpr/ppermute | solution.py:22
  27.5 14.5 %select_select_fusion.2 = (f32[32,32,1024]{2,1,0:T(8,128)}, f32[32,32,1024]{2,1,0:T(8,128)S(1)}) fusion(f32[32,32,1024]{2,1,0:T(8,128)} %get-tuple-element.515, pred[32]{0:T(512)(128)(4,1)S(1)} %fusion.40, pred[]{:T(512)S(6)} %eq.93, f32[32,1024]{1,0:T(8,128)S(1)} %get-tuple-element.537, f32[32,32,1024]{2,1,0:T(8,128)} %get-tuple-element.514, ...), kind=kLoop, calls=%fused_computation.21.clone.1 | loop fusion | flops 20971520 | bytes 18874784 | tf_op jit(solution)/shard_map/while/body/eval_jaxpr/jit(_where)/select_n | solution.py:48
  48.5 5.2 %collective-permute-start.1 = (f32[32,1,1024]{2,1,0:T(1,128)S(1)}, f32[32,1,1024]{2,1,0:T(1,128)S(1)}, u32[]{:S(2)}, u32[]{:S(2)}) collective-permute-start(f32[32,1,1024]{2,1,0:T(1,128)S(1)} %get-tuple-element.490), channel_id=1, source_target_pairs={{0,1},{1,2},{2,3},{3,4},{4,5},{5,6},{6,7},{8,9},{9,10},{10,11},{11... | collective-permute-start | bytes 393224 | tf_op jit(solution)/shard_map/while/body/eval_jaxpr/ppermute | solution.py:22
  54.8 15.5 %select_select_fusion.2 = (f32[32,32,1024]{2,1,0:T(8,128)}, f32[32,32,1024]{2,1,0:T(8,128)S(1)}) fusion(f32[32,32,1024]{2,1,0:T(8,128)} %get-tuple-element.515, pred[32]{0:T(512)(128)(4,1)S(1)} %fusion.40, pred[]{:T(512)S(6)} %eq.93, f32[32,1024]{1,0:T(8,128)S(1)} %get-tuple-element.537, f32[32,32,1024]{2,1,0:T(8,128)} %get-tuple-element.514, ...), kind=kLoop, calls=%fused_computation.21.clone.1 | loop fusion | flops 20971520 | bytes 18874784 | tf_op jit(solution)/shard_map/while/body/eval_jaxpr/jit(_where)/select_n | solution.py:48
  71.8 1.9 copy-done.1
  76.8 5.9 %collective-permute-start.1 = (f32[32,1,1024]{2,1,0:T(1,128)S(1)}, f32[32,1,1024]{2,1,0:T(1,128)S(1)}, u32[]{:S(2)}, u32[]{:S(2)}) collective-permute-start(f32[32,1,1024]{2,1,0:T(1,128)S(1)} %get-tuple-element.490), channel_id=1, source_target_pairs={{0,1},{1,2},{2,3},{3,4},{4,5},{5,6},{6,7},{8,9},{9,10},{10,11},{11... | collective-permute-start | bytes 393224 | tf_op jit(solution)/shard_map/while/body/eval_jaxpr/ppermute | solution.py:22
  83.8 15.5 %select_select_fusion.2 = (f32[32,32,1024]{2,1,0:T(8,128)}, f32[32,32,1024]{2,1,0:T(8,128)S(1)}) fusion(f32[32,32,1024]{2,1,0:T(8,128)} %get-tuple-element.515, pred[32]{0:T(512)(128)(4,1)S(1)} %fusion.40, pred[]{:T(512)S(6)} %eq.93, f32[32,1024]{1,0:T(8,128)S(1)} %get-tuple-element.537, f32[32,32,1024]{2,1,0:T(8,128)} %get-tuple-element.514, ...), kind=kLoop, calls=%fused_computation.21.clone.1 | loop fusion | flops 20971520 | bytes 18874784 | tf_op jit(solution)/shard_map/while/body/eval_jaxpr/jit(_where)/select_n | solution.py:48
  100.8 1.9 copy-done.1
  105.8 5.9 %collective-permute-start.1 = (f32[32,1,1024]{2,1,0:T(1,128)S(1)}, f32[32,1,1024]{2,1,0:T(1,128)S(1)}, u32[]{:S(2)}, u32[]{:S(2)}) collective-permute-start(f32[32,1,1024]{2,1,0:T(1,128)S(1)} %get-tuple-element.490), channel_id=1, source_target_pairs={{0,1},{1,2},{2,3},{3,4},{4,5},{5,6},{6,7},{8,9},{9,10},{10,11},{11... | collective-permute-start | bytes 393224 | tf_op jit(solution)/shard_map/while/body/eval_jaxpr/ppermute | solution.py:22
  112.8 15.5 %select_select_fusion.2 = (f32[32,32,1024]{2,1,0:T(8,128)}, f32[32,32,1024]{2,1,0:T(8,128)S(1)}) fusion(f32[32,32,1024]{2,1,0:T(8,128)} %get-tuple-element.515, pred[32]{0:T(512)(128)(4,1)S(1)} %fusion.40, pred[]{:T(512)S(6)} %eq.93, f32[32,1024]{1,0:T(8,128)S(1)} %get-tuple-element.537, f32[32,32,1024]{2,1,0:T(8,128)} %get-tuple-element.514, ...), kind=kLoop, calls=%fused_computation.21.clone.1 | loop fusion | flops 20971520 | bytes 18874784 | tf_op jit(solution)/shard_map/while/body/eval_jaxpr/jit(_where)/select_n | solution.py:48
  129.8 1.9 copy-done.1
  134.9 5.9 %collective-permute-start.1 = (f32[32,1,1024]{2,1,0:T(1,128)S(1)}, f32[32,1,1024]{2,1,0:T(1,128)S(1)}, u32[]{:S(2)}, u32[]{:S(2)}) collective-permute-start(f32[32,1,1024]{2,1,0:T(1,128)S(1)} %get-tuple-element.490), channel_id=1, source_target_pairs={{0,1},{1,2},{2,3},{3,4},{4,5},{5,6},{6,7},{8,9},{9,10},{10,11},{11... | collective-permute-start | bytes 393224 | tf_op jit(solution)/shard_map/while/body/eval_jaxpr/ppermute | solution.py:22
  141.8 15.5 %select_select_fusion.2 = (f32[32,32,1024]{2,1,0:T(8,128)}, f32[32,32,1024]{2,1,0:T(8,128)S(1)}) fusion(f32[32,32,1024]{2,1,0:T(8,128)} %get-tuple-element.515, pred[32]{0:T(512)(128)(4,1)S(1)} %fusion.40, pred[]{:T(512)S(6)} %eq.93, f32[32,1024]{1,0:T(8,128)S(1)} %get-tuple-element.537, f32[32,32,1024]{2,1,0:T(8,128)} %get-tuple-element.514, ...), kind=kLoop, calls=%fused_computation.21.clone.1 | loop fusion | flops 20971520 | bytes 18874784 | tf_op jit(solution)/shard_map/while/body/eval_jaxpr/jit(_where)/select_n | solution.py:48
  163.9 5.9 %collective-permute-start.1 = (f32[32,1,1024]{2,1,0:T(1,128)S(1)}, f32[32,1,1024]{2,1,0:T(1,128)S(1)}, u32[]{:S(2)}, u32[]{:S(2)}) collective-permute-start(f32[32,1,1024]{2,1,0:T(1,128)S(1)} %get-tuple-element.490), channel_id=1, source_target_pairs={{0,1},{1,2},{2,3},{3,4},{4,5},{5,6},{6,7},{8,9},{9,10},{10,11},{11... | collective-permute-start | bytes 393224 | tf_op jit(solution)/shard_map/while/body/eval_jaxpr/ppermute | solution.py:22
  170.8 15.5 %select_select_fusion.2 = (f32[32,32,1024]{2,1,0:T(8,128)}, f32[32,32,1024]{2,1,0:T(8,128)S(1)}) fusion(f32[32,32,1024]{2,1,0:T(8,128)} %get-tuple-element.515, pred[32]{0:T(512)(128)(4,1)S(1)} %fusion.40, pred[]{:T(512)S(6)} %eq.93, f32[32,1024]{1,0:T(8,128)S(1)} %get-tuple-element.537, f32[32,32,1024]{2,1,0:T(8,128)} %get-tuple-element.514, ...), kind=kLoop, calls=%fused_computation.21.clone.1 | loop fusion | flops 20971520 | bytes 18874784 | tf_op jit(solution)/shard_map/while/body/eval_jaxpr/jit(_where)/select_n | solution.py:48
  192.9 5.9 %collective-permute-start.1 = (f32[32,1,1024]{2,1,0:T(1,128)S(1)}, f32[32,1,1024]{2,1,0:T(1,128)S(1)}, u32[]{:S(2)}, u32[]{:S(2)}) collective-permute-start(f32[32,1,1024]{2,1,0:T(1,128)S(1)} %get-tuple-element.490), channel_id=1, source_target_pairs={{0,1},{1,2},{2,3},{3,4},{4,5},{5,6},{6,7},{8,9},{9,10},{10,11},{11... | collective-permute-start | bytes 393224 | tf_op jit(solution)/shard_map/while/body/eval_jaxpr/ppermute | solution.py:22
  199.8 15.5 %select_select_fusion.2 = (f32[32,32,1024]{2,1,0:T(8,128)}, f32[32,32,1024]{2,1,0:T(8,128)S(1)}) fusion(f32[32,32,1024]{2,1,0:T(8,128)} %get-tuple-element.515, pred[32]{0:T(512)(128)(4,1)S(1)} %fusion.40, pred[]{:T(512)S(6)} %eq.93, f32[32,1024]{1,0:T(8,128)S(1)} %get-tuple-element.537, f32[32,32,1024]{2,1,0:T(8,128)} %get-tuple-element.514, ...), kind=kLoop, calls=%fused_computation.21.clone.1 | loop fusion | flops 20971520 | bytes 18874784 | tf_op jit(solution)/shard_map/while/body/eval_jaxpr/jit(_where)/select_n | solution.py:48
  221.9 6.2 %collective-permute-start.1 = (f32[32,1,1024]{2,1,0:T(1,128)S(1)}, f32[32,1,1024]{2,1,0:T(1,128)S(1)}, u32[]{:S(2)}, u32[]{:S(2)}) collective-permute-start(f32[32,1,1024]{2,1,0:T(1,128)S(1)} %get-tuple-element.490), channel_id=1, source_target_pairs={{0,1},{1,2},{2,3},{3,4},{4,5},{5,6},{6,7},{8,9},{9,10},{10,11},{11... | collective-permute-start | bytes 393224 | tf_op jit(solution)/shard_map/while/body/eval_jaxpr/ppermute | solution.py:22
  229.0 15.5 %select_select_fusion.2 = (f32[32,32,1024]{2,1,0:T(8,128)}, f32[32,32,1024]{2,1,0:T(8,128)S(1)}) fusion(f32[32,32,1024]{2,1,0:T(8,128)} %get-tuple-element.515, pred[32]{0:T(512)(128)(4,1)S(1)} %fusion.40, pred[]{:T(512)S(6)} %eq.93, f32[32,1024]{1,0:T(8,128)S(1)} %get-tuple-element.537, f32[32,32,1024]{2,1,0:T(8,128)} %get-tuple-element.514, ...), kind=kLoop, calls=%fused_computation.21.clone.1 | loop fusion | flops 20971520 | bytes 18874784 | tf_op jit(solution)/shard_map/while/body/eval_jaxpr/jit(_where)/select_n | solution.py:48
  248.1 3.8 %multiply_reduce_fusion = f32[8,32,1024]{2,1,0:T(8,128)} fusion(f32[4,8,32,1024]{3,2,1,0:T(8,128)} %bitcast.23, f32[4]{0:T(128)S(1)} %dynamic_slice.11), kind=kLoop, calls=%fused_computation.32 | loop fusion | flops 1835008 | bytes 5242896 | tf_op jit(solution)/shard_map/reduce_sum | solution.py:108
  251.9 39.8 %reduce-scatter.2.cloned.1.call-done = f32[2,32,1024]{2,1,0:T(8,128)} async-done(((f32[8,32,1024]{2,1,0:T(8,128)}), f32[2,32,1024]{2,1,0:T(8,128)}) %reduce-scatter.2.cloned.1.call-update) | async-done | bytes 262160 | tf_op jit(solution)/shard_map/reduce_scatter | solution.py:113
  (146 shorter events, 53.9 us)
Async XLA Ops:
  6.5 285.2 %reduce-scatter.2.cloned.1.call-start = ((), (), s32[]{:S(2)}) async-start(), calls=%async_computation.1 | async-start | bytes 1310720 | tf_op jit(solution)/shard_map/reduce_scatter | solution.py:113
  7.4 10.0 %collective-permute-start.2 = (f32[1,1024]{1,0:T(1,128)S(1)}, f32[1,1024]{1,0:T(1,128)S(1)}, u32[]{:S(2)}, u32[]{:S(2)}) collective-permute-start(f32[1,1024]{1,0:T(1,128)S(1)} %get-tuple-element.392), channel_id=1, source_target_pairs={{0,1},{1,2},{2,3},{3,4},{4,5},{5,6},{6,7},{8,9},{9,10},{10,11},{11... | collective-permute-start | bytes 12296 | tf_op jit(solution)/shard_map/ppermute | solution.py:22
  9.8 7.6 %collective-permute-start.3 = (f32[1,1024]{1,0:T(1,128)S(1)}, f32[1,1024]{1,0:T(1,128)S(1)}, u32[]{:S(2)}, u32[]{:S(2)}) collective-permute-start(f32[1,1024]{1,0:T(1,128)S(1)} %get-tuple-element.393), channel_id=1, source_target_pairs={{1,0},{2,1},{3,2},{4,3},{5,4},{6,5},{7,6},{9,8},{10,9},{11,10},{12... | collective-permute-start | bytes 12296 | tf_op jit(solution)/shard_map/ppermute | solution.py:25
  19.4 7.9 %collective-permute-start = (f32[32,1,1024]{2,1,0:T(1,128)S(1)}, f32[32,1,1024]{2,1,0:T(1,128)S(1)}, u32[]{:S(2)}, u32[]{:S(2)}) collective-permute-start(f32[32,1,1024]{2,1,0:T(1,128)S(1)} %get-tuple-element.489), channel_id=1, source_target_pairs={{1,0},{2,1},{3,2},{4,3},{5,4},{6,5},{7,6},{9,8},{10,9},{11,10},{12... | collective-permute-start | bytes 393224 | tf_op jit(solution)/shard_map/while/body/eval_jaxpr/ppermute | solution.py:25
  20.7 6.7 %collective-permute-start.1 = (f32[32,1,1024]{2,1,0:T(1,128)S(1)}, f32[32,1,1024]{2,1,0:T(1,128)S(1)}, u32[]{:S(2)}, u32[]{:S(2)}) collective-permute-start(f32[32,1,1024]{2,1,0:T(1,128)S(1)} %get-tuple-element.490), channel_id=1, source_target_pairs={{0,1},{1,2},{2,3},{3,4},{4,5},{5,6},{6,7},{8,9},{9,10},{10,11},{11... | collective-permute-start | bytes 393224 | tf_op jit(solution)/shard_map/while/body/eval_jaxpr/ppermute | solution.py:22
  47.2 7.4 %collective-permute-start = (f32[32,1,1024]{2,1,0:T(1,128)S(1)}, f32[32,1,1024]{2,1,0:T(1,128)S(1)}, u32[]{:S(2)}, u32[]{:S(2)}) collective-permute-start(f32[32,1,1024]{2,1,0:T(1,128)S(1)} %get-tuple-element.489), channel_id=1, source_target_pairs={{1,0},{2,1},{3,2},{4,3},{5,4},{6,5},{7,6},{9,8},{10,9},{11,10},{12... | collective-permute-start | bytes 393224 | tf_op jit(solution)/shard_map/while/body/eval_jaxpr/ppermute | solution.py:25
  48.5 6.2 %collective-permute-start.1 = (f32[32,1,1024]{2,1,0:T(1,128)S(1)}, f32[32,1,1024]{2,1,0:T(1,128)S(1)}, u32[]{:S(2)}, u32[]{:S(2)}) collective-permute-start(f32[32,1,1024]{2,1,0:T(1,128)S(1)} %get-tuple-element.490), channel_id=1, source_target_pairs={{0,1},{1,2},{2,3},{3,4},{4,5},{5,6},{6,7},{8,9},{9,10},{10,11},{11... | collective-permute-start | bytes 393224 | tf_op jit(solution)/shard_map/while/body/eval_jaxpr/ppermute | solution.py:22
  54.8 15.5 %copy-start = (f32[32,32,1024]{2,1,0:T(8,128)S(1)}, f32[32,32,1024]{2,1,0:T(8,128)}, u32[]{:S(2)}) copy-start(f32[32,32,1024]{2,1,0:T(8,128)} %get-tuple-element.514) | copy-start | bytes 12582916 | tf_op jit(solution)/shard_map/while
  75.5 8.1 %collective-permute-start = (f32[32,1,1024]{2,1,0:T(1,128)S(1)}, f32[32,1,1024]{2,1,0:T(1,128)S(1)}, u32[]{:S(2)}, u32[]{:S(2)}) collective-permute-start(f32[32,1,1024]{2,1,0:T(1,128)S(1)} %get-tuple-element.489), channel_id=1, source_target_pairs={{1,0},{2,1},{3,2},{4,3},{5,4},{6,5},{7,6},{9,8},{10,9},{11,10},{12... | collective-permute-start | bytes 393224 | tf_op jit(solution)/shard_map/while/body/eval_jaxpr/ppermute | solution.py:25
  76.8 6.9 %collective-permute-start.1 = (f32[32,1,1024]{2,1,0:T(1,128)S(1)}, f32[32,1,1024]{2,1,0:T(1,128)S(1)}, u32[]{:S(2)}, u32[]{:S(2)}) collective-permute-start(f32[32,1,1024]{2,1,0:T(1,128)S(1)} %get-tuple-element.490), channel_id=1, source_target_pairs={{0,1},{1,2},{2,3},{3,4},{4,5},{5,6},{6,7},{8,9},{9,10},{10,11},{11... | collective-permute-start | bytes 393224 | tf_op jit(solution)/shard_map/while/body/eval_jaxpr/ppermute | solution.py:22
  83.8 15.5 %copy-start = (f32[32,32,1024]{2,1,0:T(8,128)S(1)}, f32[32,32,1024]{2,1,0:T(8,128)}, u32[]{:S(2)}) copy-start(f32[32,32,1024]{2,1,0:T(8,128)} %get-tuple-element.514) | copy-start | bytes 12582916 | tf_op jit(solution)/shard_map/while
  104.5 8.1 %collective-permute-start = (f32[32,1,1024]{2,1,0:T(1,128)S(1)}, f32[32,1,1024]{2,1,0:T(1,128)S(1)}, u32[]{:S(2)}, u32[]{:S(2)}) collective-permute-start(f32[32,1,1024]{2,1,0:T(1,128)S(1)} %get-tuple-element.489), channel_id=1, source_target_pairs={{1,0},{2,1},{3,2},{4,3},{5,4},{6,5},{7,6},{9,8},{10,9},{11,10},{12... | collective-permute-start | bytes 393224 | tf_op jit(solution)/shard_map/while/body/eval_jaxpr/ppermute | solution.py:25
  105.8 6.9 %collective-permute-start.1 = (f32[32,1,1024]{2,1,0:T(1,128)S(1)}, f32[32,1,1024]{2,1,0:T(1,128)S(1)}, u32[]{:S(2)}, u32[]{:S(2)}) collective-permute-start(f32[32,1,1024]{2,1,0:T(1,128)S(1)} %get-tuple-element.490), channel_id=1, source_target_pairs={{0,1},{1,2},{2,3},{3,4},{4,5},{5,6},{6,7},{8,9},{9,10},{10,11},{11... | collective-permute-start | bytes 393224 | tf_op jit(solution)/shard_map/while/body/eval_jaxpr/ppermute | solution.py:22
  133.6 8.1 %collective-permute-start = (f32[32,1,1024]{2,1,0:T(1,128)S(1)}, f32[32,1,1024]{2,1,0:T(1,128)S(1)}, u32[]{:S(2)}, u32[]{:S(2)}) collective-permute-start(f32[32,1,1024]{2,1,0:T(1,128)S(1)} %get-tuple-element.489), channel_id=1, source_target_pairs={{1,0},{2,1},{3,2},{4,3},{5,4},{6,5},{7,6},{9,8},{10,9},{11,10},{12... | collective-permute-start | bytes 393224 | tf_op jit(solution)/shard_map/while/body/eval_jaxpr/ppermute | solution.py:25
  134.9 6.9 %collective-permute-start.1 = (f32[32,1,1024]{2,1,0:T(1,128)S(1)}, f32[32,1,1024]{2,1,0:T(1,128)S(1)}, u32[]{:S(2)}, u32[]{:S(2)}) collective-permute-start(f32[32,1,1024]{2,1,0:T(1,128)S(1)} %get-tuple-element.490), channel_id=1, source_target_pairs={{0,1},{1,2},{2,3},{3,4},{4,5},{5,6},{6,7},{8,9},{9,10},{10,11},{11... | collective-permute-start | bytes 393224 | tf_op jit(solution)/shard_map/while/body/eval_jaxpr/ppermute | solution.py:22
  141.8 15.5 %copy-start = (f32[32,32,1024]{2,1,0:T(8,128)S(1)}, f32[32,32,1024]{2,1,0:T(8,128)}, u32[]{:S(2)}) copy-start(f32[32,32,1024]{2,1,0:T(8,128)} %get-tuple-element.514) | copy-start | bytes 12582916 | tf_op jit(solution)/shard_map/while
  162.6 8.1 %collective-permute-start = (f32[32,1,1024]{2,1,0:T(1,128)S(1)}, f32[32,1,1024]{2,1,0:T(1,128)S(1)}, u32[]{:S(2)}, u32[]{:S(2)}) collective-permute-start(f32[32,1,1024]{2,1,0:T(1,128)S(1)} %get-tuple-element.489), channel_id=1, source_target_pairs={{1,0},{2,1},{3,2},{4,3},{5,4},{6,5},{7,6},{9,8},{10,9},{11,10},{12... | collective-permute-start | bytes 393224 | tf_op jit(solution)/shard_map/while/body/eval_jaxpr/ppermute | solution.py:25
  163.9 6.9 %collective-permute-start.1 = (f32[32,1,1024]{2,1,0:T(1,128)S(1)}, f32[32,1,1024]{2,1,0:T(1,128)S(1)}, u32[]{:S(2)}, u32[]{:S(2)}) collective-permute-start(f32[32,1,1024]{2,1,0:T(1,128)S(1)} %get-tuple-element.490), channel_id=1, source_target_pairs={{0,1},{1,2},{2,3},{3,4},{4,5},{5,6},{6,7},{8,9},{9,10},{10,11},{11... | collective-permute-start | bytes 393224 | tf_op jit(solution)/shard_map/while/body/eval_jaxpr/ppermute | solution.py:22
  191.6 8.1 %collective-permute-start = (f32[32,1,1024]{2,1,0:T(1,128)S(1)}, f32[32,1,1024]{2,1,0:T(1,128)S(1)}, u32[]{:S(2)}, u32[]{:S(2)}) collective-permute-start(f32[32,1,1024]{2,1,0:T(1,128)S(1)} %get-tuple-element.489), channel_id=1, source_target_pairs={{1,0},{2,1},{3,2},{4,3},{5,4},{6,5},{7,6},{9,8},{10,9},{11,10},{12... | collective-permute-start | bytes 393224 | tf_op jit(solution)/shard_map/while/body/eval_jaxpr/ppermute | solution.py:25
  192.9 6.9 %collective-permute-start.1 = (f32[32,1,1024]{2,1,0:T(1,128)S(1)}, f32[32,1,1024]{2,1,0:T(1,128)S(1)}, u32[]{:S(2)}, u32[]{:S(2)}) collective-permute-start(f32[32,1,1024]{2,1,0:T(1,128)S(1)} %get-tuple-element.490), channel_id=1, source_target_pairs={{0,1},{1,2},{2,3},{3,4},{4,5},{5,6},{6,7},{8,9},{9,10},{10,11},{11... | collective-permute-start | bytes 393224 | tf_op jit(solution)/shard_map/while/body/eval_jaxpr/ppermute | solution.py:22
  199.8 15.5 %copy-start = (f32[32,32,1024]{2,1,0:T(8,128)S(1)}, f32[32,32,1024]{2,1,0:T(8,128)}, u32[]{:S(2)}) copy-start(f32[32,32,1024]{2,1,0:T(8,128)} %get-tuple-element.514) | copy-start | bytes 12582916 | tf_op jit(solution)/shard_map/while
  220.6 8.3 %collective-permute-start = (f32[32,1,1024]{2,1,0:T(1,128)S(1)}, f32[32,1,1024]{2,1,0:T(1,128)S(1)}, u32[]{:S(2)}, u32[]{:S(2)}) collective-permute-start(f32[32,1,1024]{2,1,0:T(1,128)S(1)} %get-tuple-element.489), channel_id=1, source_target_pairs={{1,0},{2,1},{3,2},{4,3},{5,4},{6,5},{7,6},{9,8},{10,9},{11,10},{12... | collective-permute-start | bytes 393224 | tf_op jit(solution)/shard_map/while/body/eval_jaxpr/ppermute | solution.py:25
  221.9 7.2 %collective-permute-start.1 = (f32[32,1,1024]{2,1,0:T(1,128)S(1)}, f32[32,1,1024]{2,1,0:T(1,128)S(1)}, u32[]{:S(2)}, u32[]{:S(2)}) collective-permute-start(f32[32,1,1024]{2,1,0:T(1,128)S(1)} %get-tuple-element.490), channel_id=1, source_target_pairs={{0,1},{1,2},{2,3},{3,4},{4,5},{5,6},{6,7},{8,9},{9,10},{10,11},{11... | collective-permute-start | bytes 393224 | tf_op jit(solution)/shard_map/while/body/eval_jaxpr/ppermute | solution.py:22
  229.0 15.5 %copy-start = (f32[32,32,1024]{2,1,0:T(8,128)S(1)}, f32[32,32,1024]{2,1,0:T(8,128)}, u32[]{:S(2)}) copy-start(f32[32,32,1024]{2,1,0:T(8,128)} %get-tuple-element.514) | copy-start | bytes 12582916 | tf_op jit(solution)/shard_map/while
  (15 other events, 101.9 us)
Sparse Core Ops, SparseCore 0:
  252.0 39.6 reduce-scatter.1
where the time goes:
time: 300 us; the launch traced here: 299 us
  other arithmetic  146 us (49%)
  starting transfers between devices  61 us (20%)
  waiting for transfers between devices  40.9 us (14%)
  local copies, waits for them, and re-layouts  32 us (11%)
  between operations  13.5 us (4%)
  loops' own time  5.56 us (2%)
    select_n x8, other arithmetic, chebyshev_step(): jnp.where(active, moved, direction)  123 us
    ppermute x9, starting transfers between devices, with_halo(): lax.ppermute(lax.slice_in_dim(block, block.shape[dim] - width, None, axis...  49.3 us
    reduce_scatter x1, waiting for transfers between devices, local(): return lax.psum_scatter(summed, 'wave', scatter_dimension=0, tiled=True)  39.8 us
    while x40, local copies, waits for them, and re-layouts  15.6 us
    slice x9, local copies, waits for them, and re-layouts, with_halo(): lax.slice_in_dim(block, block.shape[dim] - width, None, axis=dim)  14.9 us
    select_n x8, other arithmetic, chebyshev_step(): jnp.where(active, field + moved, field)  12.6 us
    ppermute x9, starting transfers between devices, with_halo(): lax.ppermute(lax.slice_in_dim(block, 0, width, axis=dim), axis, backward)  11.6 us
  transfers between devices with their start and end apart: 19, of which 9 were waited for; matrix products, arithmetic and copies ran while one was open for 3% of the time, Pallas kernels for 0%

commit v1 on v0

v1 whole, which is shorter than its diff:
```python
import functools

import jax
import jax.numpy as jnp
from jax import lax
from jax.experimental import pallas as pl
from jax.experimental.pallas import tpu as pltpu
from jax.sharding import PartitionSpec as P

ITERS = 8
LOWER = 0.1
UPPER = 2.0
THETA = (UPPER + LOWER) / 2.0
DELTA = (UPPER - LOWER) / 2.0
SIGMA_ONE = THETA / DELTA
CURRENT = 2.0
DIAG = 2.0 * (THETA - 1.0) / DELTA
LANES = 128
SUB = 8


def chebyshev_table():
    values = [1.0, SIGMA_ONE]
    for _ in range(ITERS):
        values.append(2.0 * SIGMA_ONE * values[-1] - values[-2])
    return values


TABLE = chebyshev_table()


def coefficients_kernel(squares, cond_lo, cond, cond_hi, c_north, c_east, root, q_first, cond_pad, q_pad):
    rows, cols = cond.shape
    halo = cond_lo.shape[0]
    tall = rows + 2 * halo
    waves = root.shape[0]
    pair = SUB // waves
    cond_pad[pl.ds(0, halo), :] = jnp.zeros((halo, cols), jnp.float32)
    cond_pad[pl.ds(halo, halo), :] = cond_lo[...]
    cond_pad[pl.ds(2 * halo, rows), :] = cond[...]
    cond_pad[pl.ds(2 * halo + rows, halo), :] = cond_hi[...]
    cond_pad[pl.ds(3 * halo + rows, halo), :] = jnp.zeros((halo, cols), jnp.float32)
    lane = lax.broadcasted_iota(jnp.int32, (SUB, cols), 1)

    def faces(base):
        mid = cond_pad[pl.ds(base, SUB), :]
        up = cond_pad[pl.ds(base - 1, SUB), :]
        down = cond_pad[pl.ds(base + 1, SUB), :]
        east = 0.5 * (mid + jnp.where(lane == cols - 1, 0.0, pltpu.roll(mid, cols - 1, 1)))
        west = 0.5 * (mid + jnp.where(lane == 0, 0.0, pltpu.roll(mid, 1, 1)))
        return mid, 0.5 * (mid + up), 0.5 * (mid + down), east, west

    q_pad[...] = jnp.zeros(q_pad.shape, jnp.float32)
    for tile in range(tall // SUB):
        base = tile * SUB
        mid, north, south, east, west = faces(halo + base)
        diagonal = north + south + west + east
        inside = mid > 0.0
        for w in range(waves):
            sq = jnp.sqrt(diagonal + squares[w] * mid)
            root[w, pl.ds(base, SUB), :] = sq
            q_pad[w, pl.ds(halo + base, SUB), :] = jnp.where(inside, 1.0 / sq, 0.0)
    for tile in range(tall // SUB):
        base = tile * SUB
        mid, north, south, east, west = faces(halo + base)
        inside = mid > 0.0
        edge = jnp.where(lane == cols - 1, 0.0, east)
        for w in range(waves):
            q = q_pad[w, pl.ds(halo + base, SUB), :]
            q_up = q_pad[w, pl.ds(halo + base - 1, SUB), :]
            scaled = (2.0 / DELTA) * q
            north_w = scaled * q_up * north
            east_w = scaled * pltpu.roll(q, cols - 1, 1) * edge
            for s in range(pair):
                spot = pl.ds(base * SUB + w * pair + s, SUB, stride=SUB)
                q_first[spot, :] = jnp.where(lane[:, :LANES] == 0, q[:, :LANES], 0.0)
                for j in range(cols // LANES):
                    c_north[j, spot, :] = north_w[:, j * LANES:(j + 1) * LANES]
                    c_east[j, spot, :] = east_w[:, j * LANES:(j + 1) * LANES]


def sweep_kernel(
    counts, levels, scale, electrodes, first_row,
    lo, own, hi, c_north, c_east, root, q_first, out, u_even, u_odd,
):
    waves, sources, rows, cols = own.shape
    halo = lo.shape[2]
    pair = SUB // waves
    chunks = sources // pair
    tall = rows + 2 * halo
    limit = levels[0]
    ids = lax.broadcasted_iota(jnp.int32, (SUB, LANES), 0)
    lanes = lax.broadcasted_iota(jnp.int32, (SUB, LANES), 1)

    width = cols // LANES

    def rows_of(ref, r):
        spot = pl.ds(pl.multiple_of(r * SUB, SUB), SUB)
        return tuple(ref[j, spot, :] for j in range(width))

    def one_chunk(c, _):
        for w in range(waves):
            for s in range(pair):
                i = w * pair + s
                for ref, start in ((lo, 0), (own, halo), (hi, halo + rows)):
                    for tile in range(ref.shape[2] // SUB):
                        base = start + tile * SUB
                        part = ref[w, c * pair + s, pl.ds(tile * SUB, SUB), :].astype(jnp.float32)
                        part = part * root[w, pl.ds(base, SUB), :]
                        for j in range(width):
                            u_even[j, pl.ds(base * SUB + i, SUB, stride=SUB), :] = (
                                part[:, j * LANES:(j + 1) * LANES]
                            )
        out[pl.ds(c * pair, pair)] = jnp.zeros((pair, rows, cols), jnp.float32)

        def level(t, src, dst, first):
            depth = limit - t
            begin = halo - depth
            boost = scale[t]

            def row(r, up, mid, north):
                down = rows_of(src, r + 1)
                south = rows_of(c_north, r + 1)
                east = rows_of(c_east, r)
                spot = pl.ds(pl.multiple_of(r * SUB, SUB), SUB)
                left = [pltpu.roll(v, LANES - 1, 1) for v in mid]
                right = [pltpu.roll(e * v, 1, 1) for e, v in zip(east, mid)]
                for j in range(width):
                    from_east = left[j] if j == width - 1 else jnp.where(lanes == LANES - 1, left[j + 1], left[j])
                    from_west = jnp.where(lanes == 0, right[j - 1], right[j])
                    total = (
                        (north[j] * up[j] + south[j] * down[j])
                        + (east[j] * from_east + from_west) + DIAG * mid[j]
                    )
                    if first:
                        total = 0.5 * total
                    else:
                        total = total - dst[j, spot, :]
                    dst[j, spot, :] = total
                return mid, down, south

            def body(k, carry):
                r = begin + 2 * k
                carry = row(r, *carry)
                return row(r + 1, *carry)

            lax.fori_loop(
                0, rows // 2 + depth, body,
                (rows_of(src, begin - 1), rows_of(src, begin), rows_of(c_north, begin)),
            )

            for s in range(pair):
                for pole, sign in ((0, 1.0), (1, -1.0)):
                    r = electrodes[(c * pair + s) * 2 + pole] - first_row[0] + halo

                    @pl.when(jnp.logical_and(r >= begin, r < begin + rows + 2 * depth))
                    def _():
                        spot = pl.ds(pl.multiple_of(r * SUB, SUB), SUB)
                        add = jnp.where(lax.rem(ids, pair) == s, q_first[spot, :], 0.0)
                        dst[0, spot, :] = dst[0, spot, :] + (sign * boost) * add

            for w in range(waves):

                @pl.when(counts[w] == t)
                def _():
                    for tile in range(rows // SUB):
                        base = halo + tile * SUB
                        factor = counts_scale(w, t) / root[w, pl.ds(base, SUB), :]
                        for s in range(pair):
                            spot = pl.ds(base * SUB + w * pair + s, SUB, stride=SUB)
                            for j in range(width):
                                here = (c * pair + s, pl.ds(tile * SUB, SUB), pl.ds(j * LANES, LANES))
                                part = factor[:, j * LANES:(j + 1) * LANES]
                                out[here] = out[here] + part * dst[j, spot, :]

        def counts_scale(w, t):
            return scale[ITERS + 1 + w] * scale[ITERS + 1 + waves + t]

        level(1, u_even, u_odd, True)

        def two(k, _):
            level(2 * k, u_odd, u_even, False)

            @pl.when(2 * k + 1 <= limit)
            def _():
                level(2 * k + 1, u_even, u_odd, False)

            return 0

        lax.fori_loop(1, limit // 2 + 1, two, 0)
        return 0

    lax.fori_loop(0, chunks, one_chunk, 0)


def local(
    initial_fields, conductivity, wavenumbers, quad_weights, sweep_counts, electrode_cells,
    source_pairs,
):
    row_count, col_count = conductivity.shape
    waves, sources = initial_fields.shape[:2]
    halo = ITERS
    tile_pos = lax.axis_index("tile")
    wave_pos = lax.axis_index("wave")
    count = lax.axis_size("tile")
    forward = [(i, i + 1) for i in range(count - 1)]
    backward = [(i + 1, i) for i in range(count - 1)]
    cond_lo = lax.ppermute(conductivity[-halo:], "tile", forward)
    cond_hi = lax.ppermute(conductivity[:halo], "tile", backward)
    lo = lax.ppermute(initial_fields[:, :, -halo:], "tile", forward)
    hi = lax.ppermute(initial_fields[:, :, :halo], "tile", backward)
    mine = lambda v: lax.dynamic_slice_in_dim(v, wave_pos * waves, waves)
    values, weights, counts = mine(wavenumbers), mine(quad_weights), mine(sweep_counts)
    electrodes = electrode_cells[source_pairs.reshape(-1)]
    sources_scale = [0.0, CURRENT / DELTA] + [2.0 * CURRENT / DELTA * TABLE[t] for t in range(1, ITERS)]
    ends = [0.0] + [1.0 / TABLE[t] for t in range(1, ITERS + 1)]
    scale = jnp.concatenate(
        [jnp.array(sources_scale, jnp.float32), weights, jnp.array(ends, jnp.float32)]
    )
    tall = row_count + 2 * halo
    smem = pl.BlockSpec(memory_space=pltpu.SMEM)
    vmem = pl.BlockSpec(memory_space=pltpu.VMEM)
    wide = jax.ShapeDtypeStruct((col_count // LANES, tall * SUB, LANES), jnp.float32)
    c_north, c_east, root, q_first = pl.pallas_call(
        coefficients_kernel,
        out_shape=(wide, wide, jax.ShapeDtypeStruct((waves, tall, col_count), jnp.float32),
                   jax.ShapeDtypeStruct((tall * SUB, LANES), jnp.float32)),
        in_specs=[smem, vmem, vmem, vmem],
        out_specs=[vmem] * 4,
        scratch_shapes=[
            pltpu.VMEM((tall + 2 * halo, col_count), jnp.float32),
            pltpu.VMEM((waves, tall + 2 * halo, col_count), jnp.float32),
        ],
        name="coefficients",
    )(values * values, cond_lo, conductivity, cond_hi)
    summed = pl.pallas_call(
        sweep_kernel,
        out_shape=jax.ShapeDtypeStruct((sources, row_count, col_count), jnp.float32),
        in_specs=[smem] * 5 + [vmem] * 7,
        out_specs=vmem,
        scratch_shapes=[pltpu.VMEM((col_count // LANES, tall * SUB, LANES), jnp.float32)] * 2,
        name="sweeps",
    )(
        counts, jnp.max(counts)[None], scale, electrodes, (tile_pos * row_count)[None],
        lo, initial_fields, hi, c_north, c_east, root, q_first,
    )
    parts = lax.all_to_all(summed.reshape((lax.axis_size("wave"), -1, row_count, col_count)), "wave", 0, 0)
    return jnp.sum(parts, axis=0)


def solution(mesh):
    placed = (P("wave", None, "tile", None), P("tile", None), P(), P(), P(), P(), P())
    return jax.shard_map(
        local, mesh=mesh, in_specs=placed, out_specs=P("wave", "tile", None), check_vma=False
    )
```

time: 300 us -> 132 us (0.44)
  other arithmetic: 146 us -> 3.36 us
  Pallas kernels: 0 us -> 81 us
  starting transfers between devices: 61 us -> 10.8 us
  waiting for transfers between devices: 40.9 us -> 0.01 us
  blocking collectives: 0 us -> 29.9 us
  local copies, waits for them, and re-layouts: 32 us -> 5.77 us
  between operations: 13.5 us -> 0.13 us
  loops' own time: 5.56 us -> 0 us
    select_n x24 -> x1, other arithmetic: 136 us -> 0.01 us  [local(): electrodes = electrode_cells[source_pairs.reshape(-1)]]
    pallas_call x0 -> x2, Pallas kernels: none -> 81 us  [the longest x1 76.9 us: local(): pl.pallas_call(sweep_kernel, out_shape=jax.ShapeDtypeStruct((sources, row...]
    ppermute x18 -> x4, starting transfers between devices: 60.9 us -> 10.8 us  [the longest x1 5.15 us: local(): lo = lax.ppermute(initial_fields[:, :, -halo:], 'tile', forward)]
    reduce_scatter x1 -> x0, waiting for transfers between devices: 39.8 us -> none  [local(): return lax.psum_scatter(summed, 'wave', scatter_dimension=0, tiled=True)]
    all_to_all x0 -> x1, blocking collectives: none -> 29.9 us  [local(): lax.all_to_all(summed.reshape((lax.axis_size('wave'), -1, row_count, col_...]
    while x40 -> x0, local copies, waits for them, and re-layouts: 15.6 us -> none
    slice x10 -> x2, local copies, waits for them, and re-layouts: 14.9 us -> 2.15 us  [the longest x1 1.31 us: local(): hi = lax.ppermute(initial_fields[:, :, :halo], 'tile', backward)]
    another operation x1 -> x0, loops' own time: 5.56 us -> none  [local(): lax.fori_loop(0, ITERS, sweep, (stacked, jnp.zeros_like(stacked), rho_sta...]
  transfers between devices with their start and end apart: 19 -> 4, of which waited for: 9 -> 0; matrix products, arithmetic and copies ran while one was open for 3% -> 4% of each run, Pallas kernels for 0% -> 3%
where the time goes in v1:
time: 132 us; the launch traced here: 131 us
  Pallas kernels  81 us (61%)
  blocking collectives  29.9 us (23%)
  starting transfers between devices  10.8 us (8%)
  local copies, waits for them, and re-layouts  5.77 us (4%)
  other arithmetic  3.36 us (3%)
    pallas_call x1, Pallas kernels, local(): pl.pallas_call(sweep_kernel, out_shape=jax.ShapeDtypeStruct((sources, row...  76.9 us
    all_to_all x1, blocking collectives, local(): lax.all_to_all(summed.reshape((lax.axis_size('wave'), -1, row_count, col_...  29.9 us
    ppermute x1, starting transfers between devices, local(): lo = lax.ppermute(initial_fields[:, :, -halo:], 'tile', forward)  5.15 us
    pallas_call x1, Pallas kernels, local(): pl.pallas_call(coefficients_kernel, out_shape=(wide, wide, jax.ShapeDtype...  4.05 us
    ppermute x1, starting transfers between devices, local(): cond_lo = lax.ppermute(conductivity[-halo:], 'tile', forward)  3.03 us
  transfers between devices with their start and end apart: 4, of which 0 were waited for; matrix products, arithmetic and copies ran while one was open for 4% of the time, Pallas kernels for 3%

profile of v1, /device:TPU:0, one launch (start us, length us, event | category | flops | bytes accessed | tf_op | source)
XLA Modules:
  0.0 130.9 jit_solution(9304476904109272668)
XLA Ops:
  0.0 0.8 fusion.3
  0.9 1.3 collective-permute-start.3
  2.2 3.0 %collective-permute-start.2 = (f32[8,1024]{1,0:T(8,128)S(1)}, f32[8,1024]{1,0:T(8,128)S(1)}, u32[]{:S(2)}, u32[]{:S(2)}) collective-permute-start(f32[8,1024]{1,0:T(8,128)S(1)} %get-tuple-element.18), channel_id=1, source_target_pairs={{0,1},{1,2},{2,3},{3,4},{4,5},{5,6},{6,7},{8,9},{9,10},{10,11},{11... | collective-permute-start | bytes 98312 | tf_op jit(solution)/shard_map/ppermute | solution.py:208
  5.2 1.3 fusion.2
  6.5 1.3 collective-permute-start.1
  7.8 5.2 %collective-permute-start = (bf16[4,8,8,1024]{3,2,1,0:T(8,128)(2,1)S(1)}, bf16[4,8,8,1024]{3,2,1,0:T(8,128)(2,1)S(1)}, u32[]{:S(2)}, u32[]{:S(2)}) collective-permute-start(bf16[4,8,8,1024]{3,2,1,0:T(8,128)(2,1)S(1)} %get-tuple-element.16), channel_id=1, source_target_pairs={{0,1},{1,2},{2,3},{3,4},{4,5},{5,6},{6,7},{8,9},{9,10},{10,11},{11... | collective-permute-start | bytes 1572872 | tf_op jit(solution)/shard_map/ppermute | solution.py:210
  13.0 0.7 dynamic-slice_multiply_fusion.squares
  13.7 0.1 dynamic_slice.10
  13.8 0.1 copy.11
  13.8 0.1 reshape.34
  13.9 1.3 fusion.1
  15.3 0.6 pad_maximum_fusion.scale
  15.9 1.2 gather_fusion
  17.1 0.0 collective-permute-done.3.cond_hi
  17.1 0.0 collective-permute-done.2.cond_lo
  17.1 0.6 copy-done.3
  17.7 0.6 copy-done.4
  18.3 4.1 %coefficients.1 = (f32[8,384,128]{2,1,0:T(8,128)}, f32[8,384,128]{2,1,0:T(8,128)}, f32[4,48,1024]{2,1,0:T(8,128)}, f32[384,128]{1,0:T(8,128)}) custom-call(f32[4]{0:T(128)} %dynamic-slice_multiply_fusion.squares, f32[8,1024]{1,0:T(8,128)} %copy-done.4, f32[32,1024]{1,0:T(8,128)} %cond.1, f32[8,1024]{1,0:T(8,128)} %copy-done.3), custom_call_target="tpu_custom_call" | custom-call | tf_op jit(solution)/shard_map/coefficients/pallas_call | solution.py:224
  22.3 0.0 collective-permute-done.lo
  22.3 0.8 copy-done.1
  23.1 0.2 copy-done.2
  23.3 76.9 %sweeps.1 = f32[8,32,1024]{2,1,0:T(8,128)} custom-call(s32[4]{0:T(128)} %get-tuple-element.14.counts, s32[1]{0:T(128)} %bitcast.levels, f32[22]{0:T(128)} %pad_maximum_fusion.scale, s32[16]{0:T(128)} %gather_fusion, s32[1]{0:T(128)} %bitcast.2.first_row, bf16[4,8,8,1024]{3,2,1,0:T(8,128)(2,1)} %copy-done.2, bf16[4,8,32,1024]{3,2,1,0:T(8,128)(2,1)} %own.1, ...), custom_call_target="tpu_custom_call" | custom-call | tf_op jit(solution)/shard_map/sweeps/pallas_call | solution.py:236
  100.2 29.9 %all_to_all.5 = f32[4,2,32,1024]{3,2,1,0:T(8,128)S(1)} all-to-all(f32[4,2,32,1024]{3,2,1,0:T(8,128)} %bitcast.5), channel_id=1, replica_groups=mesh['wave'=4,'tile'=8] {'wave'}, dimensions={0} | all-to-all | bytes 2097152 | tf_op jit(solution)/shard_map/all_to_all | solution.py:247
  130.1 0.8 reduce_sum.9
  (21 shorter events, 0.0 us)
Async XLA Ops:
  0.0 15.9 %copy-start = (s32[64]{0:T(128)S(1)}, s32[64]{0:T(128)}, u32[]{:S(2)}) copy-start(s32[64]{0:T(128)} %param.14) | copy-start | bytes 772
  0.0 15.2 %copy-start.7 = (f32[9]{0:T(128)S(1)}, f32[9]{0:T(128)}, u32[]{:S(2)}) copy-start(f32[9]{0:T(128)} %constant.28.clone) | copy-start | bytes 112
  0.0 15.3 %copy-start.8 = (f32[9]{0:T(128)S(1)}, f32[9]{0:T(128)}, u32[]{:S(2)}) copy-start(f32[9]{0:T(128)} %constant.27.clone) | copy-start | bytes 112
  0.0 13.0 %copy-start.9 = (f32[16]{0:T(128)S(1)}, f32[16]{0:T(128)}, u32[]{:S(2)}) copy-start(f32[16]{0:T(128)} %param.11) | copy-start | bytes 196
  0.0 13.7 %copy-start.10 = (f32[16]{0:T(128)S(1)}, f32[16]{0:T(128)}, u32[]{:S(2)}) copy-start(f32[16]{0:T(128)} %param.12) | copy-start | bytes 196
  0.0 13.7 %copy-start.5 = (s32[8,2]{0,1:T(2,128)S(1)}, s32[8,2]{0,1:T(2,128)}, u32[]{:S(2)}) copy-start(s32[8,2]{0,1:T(2,128)} %param.15) | copy-start | bytes 196
  0.0 13.9 %copy-start.6 = (s32[16]{0:T(128)S(1)}, s32[16]{0:T(128)}, u32[]{:S(2)}) copy-start(s32[16]{0:T(128)} %param.13) | copy-start | bytes 196
  0.9 16.2 %collective-permute-start.3 = (f32[8,1024]{1,0:T(8,128)S(1)}, f32[8,1024]{1,0:T(8,128)S(1)}, u32[]{:S(2)}, u32[]{:S(2)}) collective-permute-start(f32[8,1024]{1,0:T(8,128)S(1)} %get-tuple-element.17), channel_id=1, source_target_pairs={{1,0},{2,1},{3,2},{4,3},{5,4},{6,5},{7,6},{9,8},{10,9},{11,10},{12... | collective-permute-start | bytes 98312 | tf_op jit(solution)/shard_map/ppermute | solution.py:209
  2.2 14.9 %collective-permute-start.2 = (f32[8,1024]{1,0:T(8,128)S(1)}, f32[8,1024]{1,0:T(8,128)S(1)}, u32[]{:S(2)}, u32[]{:S(2)}) collective-permute-start(f32[8,1024]{1,0:T(8,128)S(1)} %get-tuple-element.18), channel_id=1, source_target_pairs={{0,1},{1,2},{2,3},{3,4},{4,5},{5,6},{6,7},{8,9},{9,10},{10,11},{11... | collective-permute-start | bytes 98312 | tf_op jit(solution)/shard_map/ppermute | solution.py:208
  6.5 15.8 %collective-permute-start.1 = (bf16[4,8,8,1024]{3,2,1,0:T(8,128)(2,1)S(1)}, bf16[4,8,8,1024]{3,2,1,0:T(8,128)(2,1)S(1)}, u32[]{:S(2)}, u32[]{:S(2)}) collective-permute-start(bf16[4,8,8,1024]{3,2,1,0:T(8,128)(2,1)S(1)} %get-tuple-element.15), channel_id=1, source_target_pairs={{1,0},{2,1},{3,2},{4,3},{5,4},{6,5},{7,6},{9,8},{10,9},{11,10},{12... | collective-permute-start | bytes 1572872 | tf_op jit(solution)/shard_map/ppermute | solution.py:211
  7.8 14.5 %collective-permute-start = (bf16[4,8,8,1024]{3,2,1,0:T(8,128)(2,1)S(1)}, bf16[4,8,8,1024]{3,2,1,0:T(8,128)(2,1)S(1)}, u32[]{:S(2)}, u32[]{:S(2)}) collective-permute-start(bf16[4,8,8,1024]{3,2,1,0:T(8,128)(2,1)S(1)} %get-tuple-element.16), channel_id=1, source_target_pairs={{0,1},{1,2},{2,3},{3,4},{4,5},{5,6},{6,7},{8,9},{9,10},{10,11},{11... | collective-permute-start | bytes 1572872 | tf_op jit(solution)/shard_map/ppermute | solution.py:210
  17.1 0.6 copy-start.3
  17.7 0.6 copy-start.4
  22.3 0.8 copy-start.1
  22.3 1.0 copy-start.2
